TPU v7x, 512 devices: a whole 4x4x16 slice. The times are simulated.
512 devices in a mesh: row: 8 (over z_hi, core), col: 16 (over x, y), fsdp: 4 (over z_lo).
Axes of the slice: x: 4, y: 4, z: 16 (z_hi: 4, z_lo: 4; z = z_hi * 4 + z_lo), core: 2. Of those that a mesh axis runs over, the one named last changes fastest.
Arguments:
- layer_inputs: bfloat16 [4096, 8192], P('col', ('row', 'fsdp')), may hold values from -6 to 6
- output_grads: bfloat16 [4096, 14336], P(('row', 'fsdp'), 'col'), may hold values from -0.09375 to 0.09375
- weight: bfloat16 [8192, 14336], P(('row', 'fsdp'), 'col'), may hold values from -3 to 3
- moment: bfloat16 [8192, 14336], P(('row', 'fsdp'), 'col'), may hold values from -1.796875 to 1.796875
- variance: bfloat16 [8192, 14336], P(('row', 'fsdp'), 'col'), may hold values from 0.049804688 to 1
- keep_mask: int32 [64, 112], replicated, may hold values from 0 to 1, as said below
Outputs:
- new_weight: bfloat16 [8192, 14336], P(('row', 'fsdp'), 'col')
- new_moment: bfloat16 [8192, 14336], P(('row', 'fsdp'), 'col')
- new_variance: bfloat16 [8192, 14336], P(('row', 'fsdp'), 'col')
Inputs may be any that keep to these rules, and one draw needn't show every extreme that they name: `keep_mask`: 1 keeps a block of 128 x 128 weights, 0 drops it.
All inputs are finite; a program needn't handle non-finite values.
Results may differ from a plain program's by a relative error of at most 0.0039.
Values may be sent and summed in bfloat16 or wider, within the bound.
A program may use at most 128 MiB of HBM per device.

v0:
```python
import jax
import jax.numpy as jnp
from jax import lax
from jax.sharding import PartitionSpec as P

BS = 128
learn_rate = 0.02
beta_one = 0.9
beta_two = 0.95
epsilon = 1e-08
decay_rate = 0.1
first_fix = 1.0 - 0.9**10
second_fix = 1.0 - 0.95**10


def expand_keep(keep_tile):
    block_rows, block_cols = keep_tile.shape
    grid = jnp.broadcast_to(keep_tile[:, None, :, None], (block_rows, BS, block_cols, BS))
    return grid.reshape(block_rows * BS, block_cols * BS) > 0


def block_product(left_cols, right_cols):
    return lax.dot_general(
        left_cols, right_cols, (((0,), (0,)), ((), ())), preferred_element_type=jnp.float32
    )


def adam_update(grad, weight, moment, variance, keep_elem):
    weight_wide = weight.astype(jnp.float32)
    first = beta_one * moment.astype(jnp.float32) + (1.0 - beta_one) * grad
    second = beta_two * variance.astype(jnp.float32) + (1.0 - beta_two) * grad * grad
    direction = (
        first / first_fix / (jnp.sqrt(second / second_fix) + epsilon) + decay_rate * weight_wide
    )
    new_weight = jnp.where(
        keep_elem, (weight_wide - learn_rate * direction).astype(jnp.bfloat16), weight
    )
    new_moment = jnp.where(keep_elem, first.astype(jnp.bfloat16), moment)
    new_variance = jnp.where(keep_elem, second.astype(jnp.bfloat16), variance)
    return (new_weight, new_moment, new_variance)


def per_device(layer_inputs, output_grads, weight, moment, variance, keep_mask):
    fsdp_count = lax.axis_size("fsdp")
    rank_row = lax.axis_index("row")
    rank_col = lax.axis_index("col")
    rank_fsdp = lax.axis_index("fsdp")
    local_rows = weight.shape[0]
    local_cols = weight.shape[1]
    row_blocks = local_rows // BS
    col_blocks = local_cols // BS
    tile_keep = lax.dynamic_slice(
        keep_mask,
        ((rank_row * fsdp_count + rank_fsdp) * row_blocks, rank_col * col_blocks),
        (row_blocks, col_blocks),
    )
    grads_all = lax.all_gather(output_grads, ("row", "fsdp"), axis=0, tiled=True)
    grad = block_product(lax.all_gather(layer_inputs, "col", axis=0, tiled=True), grads_all)
    keep_elem = expand_keep(tile_keep)
    return adam_update(grad, weight, moment, variance, keep_elem)


def solution(mesh):
    placed = (
        P("col", ("row", "fsdp")),
        P(("row", "fsdp"), "col"),
        P(("row", "fsdp"), "col"),
        P(("row", "fsdp"), "col"),
        P(("row", "fsdp"), "col"),
        P(),
    )
    return jax.shard_map(
        per_device,
        mesh=mesh,
        in_specs=placed,
        out_specs=(P(("row", "fsdp"), "col"), P(("row", "fsdp"), "col"), P(("row", "fsdp"), "col")),
        check_vma=False,
    )
```

profile of v0, /device:TPU:1, one launch (start us, length us, event | category | flops | bytes accessed | tf_op | source)
XLA Modules:
  0.0 235.8 jit_solution(5885897363916849226)
XLA Ops:
  7.2 0.0 all-gather.3.cloned.1.call-start
  7.2 0.7 all-gather.3.cloned.1.call-update
  7.9 0.0 all-gather.5.cloned.1.call-start
  7.9 0.7 all-gather.5.cloned.1.call-update
  8.7 0.8 dynamic-slice_compare_fusion
  9.4 65.5 %all-gather.3.cloned.1.call-done = bf16[4096,256]{1,0:T(8,128)(2,1)} async-done(((bf16[256,256]{1,0:T(8,128)(2,1)}), bf16[4096,256]{1,0:T(8,128)(2,1)}) %all-gather.3.cloned.1.call-update) | async-done | bytes 2097168 | tf_op jit(solution)/shard_map/all_gather | solution.py:58
  75.0 145.1 %all-gather.5.cloned.1.call-done = bf16[4096,896]{1,0:T(8,128)(2,1)} async-done(((bf16[128,896]{1,0:T(8,128)(2,1)}), bf16[4096,896]{1,0:T(8,128)(2,1)}) %all-gather.5.cloned.1.call-update) | async-done | bytes 7340048 | tf_op jit(solution)/shard_map/all_gather | solution.py:57
  220.1 0.1 broadcast_in_dim.2
  220.2 8.8 %bitcast_select_fusion = (bf16[256,896]{1,0:T(8,128)(2,1)}, bf16[256,896]{1,0:T(8,128)(2,1)}, bf16[256,896]{1,0:T(8,128)(2,1)}) fusion(bf16[256,896]{1,0:T(8,128)(2,1)} %param.10, pred[32,8,7,128]{3,2,1,0:T(8,128)(4,1)S(1)} %bitcast.8, bf16[256,896]{1,0:T(8,128)(2,1)} %param.8, bf16[256,896]{1,0:T(8,128)(2,1)} %param.9, ...), kind=kOutput, calls=%fused_computation.8 | convolution fusion | flops 1884553216 | bytes 12419072 | tf_op jit(solution)/shard_map/dot_general | solution.py:23
Async XLA Ops:
  7.2 67.8 %all-gather.3.cloned.1.call-start = ((), (), s32[]{:S(2)}) async-start(), calls=%async_computation | async-start | bytes 2228224 | tf_op jit(solution)/shard_map/all_gather | solution.py:58
  7.9 212.2 %all-gather.5.cloned.1.call-start = ((), (), s32[]{:S(2)}) async-start(), calls=%async_computation.1 | async-start | bytes 7569408 | tf_op jit(solution)/shard_map/all_gather | solution.py:57
Sparse Core Ops, SparseCore 0:
  11.0 63.9 all-gather.2
  77.0 142.9 all-gather.4
where the time goes:
time: 236 us
  waiting for transfers between devices  212 us (90%)
  between operations  14 us (6%)
  matrix products  8.78 us (4%)
    all_gather x1, waiting for transfers between devices, per_device(): lax.all_gather(output_grads, ('row', 'fsdp'), axis=0, tiled=True)  145 us
    all_gather x1, waiting for transfers between devices, per_device(): lax.all_gather(layer_inputs, 'col', axis=0, tiled=True)  65.5 us
    dot_general x1, matrix products, block_product(): lax.dot_general(left_cols, right_cols, (((0,), (0,)), ((), ())), preferre...  8.78 us
  transfers between devices with their start and end apart: 2, of which 2 were waited for; matrix products, arithmetic and copies ran while one was open for 0% of the time, Pallas kernels for 0%

commit v1 on v0

--- a/solution.py
+++ b/solution.py
@@ -55,7 +55,15 @@
         (row_blocks, col_blocks),
     )
     grads_all = lax.all_gather(output_grads, ("row", "fsdp"), axis=0, tiled=True)
-    grad = block_product(lax.all_gather(layer_inputs, "col", axis=0, tiled=True), grads_all)
+    grad = block_product(
+        jnp.concatenate(
+            lax.all_to_all(
+                jnp.stack([layer_inputs for _ in range(lax.axis_size("col"))], 0), "col", 0, 0
+            ),
+            0,
+        ),
+        grads_all,
+    )
     keep_elem = expand_keep(tile_keep)
     return adam_update(grad, weight, moment, variance, keep_elem)
 

time: 236 us -> 172 us (0.73)
  waiting for transfers between devices: 212 us -> 139 us
  starting transfers between devices: 0.08 us -> 7.74 us
  local copies, waits for them, and re-layouts: 0.14 us -> 2.65 us
    all_gather x1 -> x0, waiting for transfers between devices: 65.5 us -> none  [per_device(): lax.all_gather(layer_inputs, 'col', axis=0, tiled=True)]
    all_gather x1, waiting for transfers between devices: 145 us -> 114 us  [per_device(): lax.all_gather(output_grads, ('row', 'fsdp'), axis=0, tiled=True)]
    all_to_all x0 -> x1, waiting for transfers between devices: none -> 24.7 us  [per_device(): lax.all_to_all(jnp.stack([layer_inputs for _ in range(lax.axis_size('col'...]
    all_to_all x0 -> x1, starting transfers between devices: none -> 7.7 us  [per_device(): lax.all_to_all(jnp.stack([layer_inputs for _ in range(lax.axis_size('col'...]
    another operation x0 -> x1, local copies, waits for them, and re-layouts: none -> 2.5 us  [per_device(): jnp.stack([layer_inputs for _ in range(lax.axis_size('col'))], 0)]
  transfers between devices with their start and end apart: 2 -> 2, of which waited for: 2 -> 2; matrix products, arithmetic and copies ran while one was open for 0% -> 2% of each run, Pallas kernels for 0% -> 0%
where the time goes in v1:
time: 172 us
  waiting for transfers between devices  139 us (81%)
  between operations  14.1 us (8%)
  starting transfers between devices  7.74 us (4%)
  matrix products  7.41 us (4%)
  local copies, waits for them, and re-layouts  2.65 us (2%)
    all_gather x1, waiting for transfers between devices, per_device(): lax.all_gather(output_grads, ('row', 'fsdp'), axis=0, tiled=True)  114 us
    all_to_all x1, waiting for transfers between devices, per_device(): lax.all_to_all(jnp.stack([layer_inputs for _ in range(lax.axis_size('col'...  24.7 us
    all_to_all x1, starting transfers between devices, per_device(): lax.all_to_all(jnp.stack([layer_inputs for _ in range(lax.axis_size('col'...  7.7 us
    dot_general x1, matrix products, block_product(): lax.dot_general(left_cols, right_cols, (((0,), (0,)), ((), ())), preferre...  7.41 us
  transfers between devices with their start and end apart: 2, of which 2 were waited for; matrix products, arithmetic and copies ran while one was open for 2% of the time, Pallas kernels for 0%

profile of v1, /device:TPU:1, one launch (start us, length us, event | category | flops | bytes accessed | tf_op | source)
XLA Modules:
  0.0 172.0 jit_solution(15847445086680285053)
XLA Ops:
  7.2 0.0 all-gather.2.cloned.1.call-start
  7.2 0.7 all-gather.2.cloned.1.call-update
  7.9 2.5 %stack.2 = bf16[16,256,256]{2,1,0:T(8,128)(2,1)} broadcast(bf16[256,256]{1,0:T(8,128)(2,1)} %param.6), dimensions={1,2} | broadcast | bytes 2228224 | tf_op jit(solution)/shard_map/stack | solution.py:61
  10.4 0.0 copy-start
  10.4 0.0 copy-start.1
  10.4 0.0 copy-start.2
  10.4 7.7 %all-to-all-start = ((bf16[16,256,256]{2,1,0:T(8,128)(2,1)}), bf16[16,256,256]{2,1,0:T(8,128)(2,1)S(1)}, u32[]{:S(2)}, u32[]{:S(2)}) async-start(bf16[16,256,256]{2,1,0:T(8,128)(2,1)} %stack.2), calls=%async_computation | async-start | bytes 4194304 | tf_op jit(solution)/shard_map/all_to_all | solution.py:60
  18.1 0.8 dynamic-slice_compare_fusion
  18.9 24.7 %all-to-all-done = bf16[16,256,256]{2,1,0:T(8,128)(2,1)S(1)} async-done(((bf16[16,256,256]{2,1,0:T(8,128)(2,1)}), bf16[16,256,256]{2,1,0:T(8,128)(2,1)S(1)}, u32[]{:S(2)}, u32[]{:S(2)}) %all-to-all-start) | async-done | bytes 2097184 | tf_op jit(solution)/shard_map/all_to_all | solution.py:60
  43.6 114.0 %all-gather.2.cloned.1.call-done = bf16[4096,896]{1,0:T(8,128)(2,1)} async-done(((bf16[128,896]{1,0:T(8,128)(2,1)}), bf16[4096,896]{1,0:T(8,128)(2,1)}) %all-gather.2.cloned.1.call-update) | async-done | bytes 7340048 | tf_op jit(solution)/shard_map/all_gather | solution.py:57
  157.6 0.1 broadcast_in_dim.2
  157.7 0.0 copy-done
  157.8 0.0 copy-done.1
  157.8 0.0 copy-done.2
  157.8 7.4 %bitcast_select_fusion = (bf16[256,896]{1,0:T(8,128)(2,1)}, bf16[256,896]{1,0:T(8,128)(2,1)}, bf16[256,896]{1,0:T(8,128)(2,1)}) fusion(bf16[256,896]{1,0:T(8,128)(2,1)S(1)} %copy-done, pred[32,8,7,128]{3,2,1,0:T(8,128)(4,1)S(1)} %bitcast.10, bf16[256,896]{1,0:T(8,128)(2,1)S(1)} %copy-done.1, bf16[256,896]{1,0:T(8,128)(2,1)S(1)} %copy-done.2, ...), kind=kOutput, calls=%fused_computation.8 | convolution fusion | flops 1884553216 | bytes 12419072 | tf_op jit(solution)/shard_map/dot_general | solution.py:23
Async XLA Ops:
  7.2 150.4 %all-gather.2.cloned.1.call-start = ((), (), s32[]{:S(2)}) async-start(), calls=%async_computation.1 | async-start | bytes 7569408 | tf_op jit(solution)/shard_map/all_gather | solution.py:57
  10.4 147.3 %copy-start = (bf16[256,896]{1,0:T(8,128)(2,1)S(1)}, bf16[256,896]{1,0:T(8,128)(2,1)}, u32[]{:S(2)}) copy-start(bf16[256,896]{1,0:T(8,128)(2,1)} %param.10) | copy-start | bytes 1376260
  10.4 147.3 %copy-start.1 = (bf16[256,896]{1,0:T(8,128)(2,1)S(1)}, bf16[256,896]{1,0:T(8,128)(2,1)}, u32[]{:S(2)}) copy-start(bf16[256,896]{1,0:T(8,128)(2,1)} %param.8) | copy-start | bytes 1376260
  10.4 147.4 %copy-start.2 = (bf16[256,896]{1,0:T(8,128)(2,1)S(1)}, bf16[256,896]{1,0:T(8,128)(2,1)}, u32[]{:S(2)}) copy-start(bf16[256,896]{1,0:T(8,128)(2,1)} %param.9) | copy-start | bytes 1376260
  10.4 33.1 %all-to-all-start = ((bf16[16,256,256]{2,1,0:T(8,128)(2,1)}), bf16[16,256,256]{2,1,0:T(8,128)(2,1)S(1)}, u32[]{:S(2)}, u32[]{:S(2)}) async-start(bf16[16,256,256]{2,1,0:T(8,128)(2,1)} %stack.2), calls=%async_computation | async-start | bytes 4194304 | tf_op jit(solution)/shard_map/all_to_all | solution.py:60
Sparse Core Ops, SparseCore 0:
  10.0 147.5 all-gather.1
